TPU v7x, 32 devices: a whole 2x2x4 slice. The times are simulated.
32 devices in a mesh: groups: 2 (over y), patch: 8 (over z, x), req: 2 (over core).
Axes of the slice: x: 2, y: 2, z: 4, core: 2. Of those that a mesh axis runs over, the one named last changes fastest.
Arguments:
- hidden: float32 [16, 8, 64, 1280], P(('groups', 'req'), 'patch'), parts along dimension 0
- skip: float32 [16, 8, 64, 1280], P(('groups', 'req'), 'patch'), parts along dimension 0, may hold values from -6 to 6
- timestep_embedding_table: float32 [50, 1280], replicated, may hold values from -5 to 5
- timesteps: int32 [16], P(('groups', 'req')), parts along dimension 0, may hold values from 0 to 49, as said below
- group_norm_gain: float32 [1280], replicated, may hold values from 0.1 to 1.9
- group_norm_bias: float32 [1280], replicated, may hold values from -3 to 3
- kernel_weight: bfloat16 [9, 1280, 1280], P(None, 'patch', 'req'), may hold values from -0.0546875 to 0.0546875
- adapter_down_weight: bfloat16 [32, 64, 11520], P(('groups', 'patch')), parts along dimension 0, may hold values from -0.0546875 to 0.0546875
- adapter_up_weight: bfloat16 [32, 64, 1280], P(('groups', 'patch')), parts along dimension 0, may hold values from -0.75 to 0.75
- request_adapter: int32 [16], P(('groups', 'req')), parts along dimension 0, may hold values from 0 to 15
- adapter_row_table: int32 [32], P('groups'), parts along dimension 0, may hold values from 0 to 15, each once
Outputs:
- block_out: float32 [16, 8, 64, 1280], P(('groups', 'req'), 'patch'), parts along dimension 0
There are 2 independent parts, one for each index of `groups`. A program takes and returns all parts, laid end to end along the dimension named above; an argument that names none is the same for every part. Nothing has to cross between parts.
Inputs may be any that keep to these rules, and one draw needn't show every extreme that they name: adapter_row_table[a] is the store row of adapter a; every row is used once. Requests 0 and 1 have different timesteps.
All inputs are finite; a program needn't handle non-finite values.
Results may differ from a plain program's by a relative error of at most 0.0026.
Values may be sent and summed in bfloat16 or wider, within the bound.
A program may use at most 128 MiB of HBM per device.

v0:
```python
import jax
import jax.numpy as jnp
from jax import lax
from jax.sharding import PartitionSpec as P

GROUPS = 32


def broadcast(block, axis, owner):
    block = jnp.where(lax.axis_index(axis) == owner, block, jnp.zeros_like(block))
    return lax.psum(block, axis)


def padded(cells, sides, width):
    for axis, dim in sides:
        count = lax.axis_size(axis)
        ends = count - 1
        head = lax.slice_in_dim(cells, 0, width, axis=dim)
        tail = lax.slice_in_dim(cells, cells.shape[dim] - width, cells.shape[dim], axis=dim)
        cells = jnp.concatenate(
            [
                lax.ppermute(tail, axis, [(i, (i + 1) % count) for i in range(ends)]),
                cells,
                lax.ppermute(head, axis, [((i + 1) % count, i) for i in range(ends)]),
            ],
            axis=dim,
        )
    return cells


def from_partner(x, axis, stride):
    return lax.ppermute(x, axis, [(i, i ^ 1 << stride) for i in range(lax.axis_size(axis))])


def make_taps(extended, rows, width):
    pieces = [extended[:, dy : dy + rows, dx : dx + width, :] for dy in range(3) for dx in range(3)]
    stacked = jnp.stack(pieces, axis=3)
    count = stacked.shape[0] * rows * width
    return stacked.reshape(count, 9, stacked.shape[-1])


def load_adapter_factors(
    adapter_down_weight, adapter_up_weight, request_adapter, adapter_row_table, request_total
):
    resident_count = adapter_down_weight.shape[0]
    fetched = []
    for request in range(request_total):
        resident_row = adapter_row_table[request_adapter[request]]
        owner = resident_row // resident_count
        store_position = resident_row % resident_count
        resident_down = lax.dynamic_index_in_dim(
            adapter_down_weight, store_position, 0, keepdims=False
        )
        resident_up = lax.dynamic_index_in_dim(adapter_up_weight, store_position, 0, keepdims=False)
        fetched.append(
            (broadcast(resident_down, "patch", owner), broadcast(resident_up, "patch", owner))
        )
    return fetched


def shards(
    hidden,
    skip,
    timestep_embedding_table,
    timesteps,
    group_norm_gain,
    group_norm_bias,
    kernel_weight,
    adapter_down_weight,
    adapter_up_weight,
    request_adapter,
    adapter_row_table,
):
    request_total, rows, width, chans = hidden.shape
    steps_count = timestep_embedding_table.shape[0]
    onehot = (timesteps[:, None] == jnp.arange(steps_count, dtype=jnp.int32)[None, :]).astype(
        jnp.float32
    )
    temb = jnp.dot(
        onehot,
        timestep_embedding_table,
        preferred_element_type=jnp.float32,
        precision=lax.Precision.HIGHEST,
    )
    shifted = hidden + temb[:, None, None, :]
    grouped = shifted.reshape(request_total, rows, width, GROUPS, chans // GROUPS)
    count = rows * lax.axis_size("patch") * width * (chans // GROUPS)
    totals = lax.psum(jnp.sum(grouped, axis=(1, 2, 4)), "patch")
    mean = totals / count
    centered = grouped - mean[:, None, None, :, None]
    squares = lax.psum(jnp.sum(centered * centered, axis=(1, 2, 4)), "patch")
    var = squares / count
    normed = (centered * lax.rsqrt(var + 1e-05)[:, None, None, :, None]).reshape(
        request_total, rows, width, chans
    )
    act = jax.nn.silu(normed * group_norm_gain + group_norm_bias).astype(jnp.bfloat16)
    extended = padded(act, (("patch", 1),), 1)
    extended = jnp.pad(extended, ((0, 0), (0, 0), (1, 1), (0, 0)))
    partner = from_partner(extended, "req", 0)
    taps = make_taps(jnp.concatenate([extended, partner], axis=0), rows, width)
    pixels = request_total * rows * width
    conv_half = jnp.einsum(
        "ptc,tco->po",
        taps,
        lax.all_gather(kernel_weight, "patch", axis=1, tiled=True),
        preferred_element_type=jnp.float32,
    )
    own_half = conv_half[:pixels]
    returned = from_partner(conv_half[pixels:], "req", 0)
    first = lax.axis_index("req") == 0
    left_half = jnp.where(first, own_half, returned)
    right_half = jnp.where(first, returned, own_half)
    conv = jnp.concatenate([left_half, right_half], axis=1).reshape(
        request_total, rows * width, chans
    )
    own_taps = taps[:pixels].reshape(request_total, rows * width, 9 * chans)
    adapter_factors = load_adapter_factors(
        adapter_down_weight, adapter_up_weight, request_adapter, adapter_row_table, request_total
    )
    deltas = []
    for request in range(request_total):
        down_factor, upper_limit = adapter_factors[request]
        low = lax.dot_general(
            own_taps[request],
            down_factor,
            (((1,), (1,)), ((), ())),
            preferred_element_type=jnp.float32,
        ).astype(jnp.bfloat16)
        deltas.append(jnp.dot(low, upper_limit, preferred_element_type=jnp.float32))
    total = conv + jnp.stack(deltas, axis=0)
    return skip + total.reshape(request_total, rows, width, chans)


def solution(mesh):
    return jax.shard_map(
        shards,
        mesh=mesh,
        in_specs=(
            P(("groups", "req"), "patch", None, None),
            P(("groups", "req"), "patch", None, None),
            P(),
            P(("groups", "req")),
            P(),
            P(),
            P(None, "patch", "req"),
            P(("groups", "patch"), None, None),
            P(("groups", "patch"), None, None),
            P(("groups", "req")),
            P("groups"),
        ),
        out_specs=P(("groups", "req"), "patch", None, None),
        check_vma=False,
    )
```

profile of v0, /device:TPU:25, one launch (start us, length us, event | category | flops | bytes accessed | tf_op | source)
XLA Modules:
  0.0 515.0 jit_solution(13756354301383934993)
XLA Ops:
  6.5 1.5 fusion.27
  15.8 1.5 fusion.26
  27.7 5.8 %select_bitcast_fusion.3 = (bf16[64,11520]{1,0:T(8,128)(2,1)}, bf16[64,11520]{1,0:T(8,128)(2,1)}, bf16[64,11520]{1,0:T(8,128)(2,1)}, bf16[64,11520]{1,0:T(8,128)(2,1)}) fusion(bf16[2,64,11520]{2,1,0:T(8,128)(2,1)} %param.18, s32[]{:T(128)S(6)} %select_n.157, pred[]{:T(512)S(6)} %eq.41, s32[]{:T(128)S(6)} %select_n.167, pred[]{:T(512)S(6)} %eq.42, ...), kind=kLoop, calls=%fused_computation.31 | loop fusion | flops 2949120 | bytes 11796500 | tf_op jit(solution)/shard_map/jit(_where)/select_n | solution.py:10
  33.5 0.8 select_bitcast_fusion.7
  34.4 0.7 all-gather.2.cloned.1.call-update
  36.0 13.8 %psum.70 = f32[4,32]{1,0:T(4,128)S(1)} all-reduce(f32[4,32]{1,0:T(4,128)S(1)} %reduce_sum.25), channel_id=1, replica_groups=mesh['groups'=2,'patch'=8,'req'=2] {'patch'}, use_global_device_ids=true, to_apply=%region_2.0 | all-reduce | flops 128 | bytes 1024 | tf_op jit(solution)/shard_map/psum | solution.py:88
  50.5 16.2 %psum.71 = f32[4,32]{1,0:T(4,128)S(1)} all-reduce(f32[4,32]{1,0:T(4,128)S(1)} %reduce_sum.37), channel_id=1, replica_groups=mesh['groups'=2,'patch'=8,'req'=2] {'patch'}, use_global_device_ids=true, to_apply=%region_5.6 | all-reduce | flops 128 | bytes 1024 | tf_op jit(solution)/shard_map/psum | solution.py:91
  66.9 0.5 multiply_convert_fusion
  67.4 4.0 collective-permute-start
  71.4 2.4 collective-permute-start.1
  73.8 41.8 %collective-permute-done = bf16[4,1,64,1280]{3,2,1,0:T(8,128)(2,1)S(1)} collective-permute-done((bf16[4,1,64,1280]{3,2,1,0:T(8,128)(2,1)S(1)}, bf16[4,1,64,1280]{3,2,1,0:T(8,128)(2,1)S(1)}, u32[]{:S(2)}, u32[]{:S(2)}) %collective-permute-start) | collective-permute-done | bytes 655392 | tf_op jit(solution)/shard_map/ppermute | solution.py:22
  115.6 0.8 fusion.5
  116.3 7.0 %collective-permute-start.2 = (bf16[4,3,66,1280]{3,2,1,0:T(8,128)(2,1)S(1)}, bf16[4,3,66,1280]{3,2,1,0:T(8,128)(2,1)}, u32[]{:S(2)}, u32[]{:S(2)}) collective-permute-start(bf16[4,3,66,1280]{3,2,1,0:T(8,128)(2,1)S(1)} %fusion.5), channel_id=1, source_target_pairs={{0,1},{1,0},{2,3},{3,2},{4,5},{5,4},{6,7},{7,6},{8,9},{9,8},{10,11... | collective-permute-start | bytes 6082568 | tf_op jit(solution)/shard_map/ppermute | solution.py:32
  123.3 4.1 collective-permute-done.2
  127.4 1.3 bitcast_dynamic-update-slice_fusion.7
  128.7 1.5 bitcast_dynamic-update-slice_fusion.6
  130.2 1.5 bitcast_dynamic-update-slice_fusion.5
  131.6 1.3 bitcast_dynamic-update-slice_fusion.4
  132.9 1.5 bitcast_dynamic-update-slice_fusion.3
  134.4 1.5 bitcast_dynamic-update-slice_fusion.2
  135.9 1.5 bitcast_dynamic-update-slice_fusion.1
  137.4 1.5 bitcast_dynamic-update-slice_fusion
  138.8 1.5 bitcast_dynamic-update-slice_fusion.8
  140.3 4.3 copy-done.3
  144.6 3.1 fusion.25
  147.7 1.2 copy.55
  148.9 1.2 copy.56
  150.3 1.2 constant_dynamic-update-slice_fusion.8
  151.5 1.1 constant_dynamic-update-slice_fusion.7
  152.7 1.2 constant_dynamic-update-slice_fusion.6
  153.8 1.2 constant_dynamic-update-slice_fusion.5
  155.0 1.2 constant_dynamic-update-slice_fusion.4
  156.2 1.2 constant_dynamic-update-slice_fusion.3
  157.3 1.2 constant_dynamic-update-slice_fusion.2
  158.5 1.2 constant_dynamic-update-slice_fusion.1
  159.7 1.2 constant_dynamic-update-slice_fusion
  160.9 111.4 %all-reduce.4.cloned.1.call-done = (bf16[64,1280]{1,0:T(8,128)(2,1)}, bf16[64,11520]{1,0:T(8,128)(2,1)}, bf16[64,1280]{1,0:T(8,128)(2,1)}, bf16[64,11520]{1,0:T(...) async-done(((bf16[64,1280]{1,0:T(8,128)(2,1)}, bf16[64,11520]{1,0:T(8,128)(2,1)}, ...) | async-done | bytes 6553616 | tf_op jit(solution)/shard_map/psum | solution.py:11
  272.3 3.3 convolution_bitcast_fusion.3
  275.6 201.0 %all-gather.2.cloned.1.call-done = bf16[9,1280,640]{2,1,0:T(8,128)(2,1)} async-done(((bf16[9,160,640]{2,1,0:T(8,128)(2,1)}), bf16[9,1280,640]{2,1,0:T(8,128)(2,1)}) %all-gather.2.cloned.1.call-update) | async-done | bytes 14745616 | tf_op jit(solution)/shard_map/all_gather | solution.py:105
  476.6 16.5 %convolution_bitcast_fusion.4 = f32[512,640]{1,0:T(8,128)S(1)} fusion(bf16[512,9,1280]{2,0,1:T(8,128)(2,1)} %constant_dynamic-update-slice_fusion, bf16[9,1280,640]{2,1,0:T(8,128)(2,1)} %all-gather.2.cloned.1.call-done), kind=kOutput, calls=%fused_computation.32 | convolution fusion | flops 7549747200 | bytes 27852800 | tf_op jit(solution)/shard_map/ptc,tco->po/dot_general | solution.py:102
  493.2 1.0 copy-done.9
  494.2 0.9 slice.103
  495.6 3.3 convolution_bitcast_fusion.2
  498.9 2.9 convolution_bitcast_fusion.1
  501.9 2.2 convolution_bitcast_fusion
  504.1 1.2 slice_select_fusion.1
  505.5 1.2 copy-done.4
  506.9 1.3 fusion.14
  (53 shorter events, 2.8 us)
Async XLA Ops:
  6.5 28.6 %copy-start = (f32[50,1280]{1,0:T(8,128)S(1)}, f32[50,1280]{1,0:T(8,128)}, u32[]{:S(2)}) copy-start(f32[50,1280]{1,0:T(8,128)} %param.13) | copy-start | bytes 768004
  6.5 265.7 %all-reduce.4.cloned.1.call-start = ((), (), s32[]{:S(2)}) async-start(), calls=%async_computation.1 | async-start | bytes 13107200 | tf_op jit(solution)/shard_map/psum | solution.py:11
  27.7 5.8 %copy-start.8 = (bf16[2,64,1280]{2,1,0:T(8,128)(2,1)S(1)}, bf16[2,64,1280]{2,1,0:T(8,128)(2,1)}, u32[]{:S(2)}) copy-start(bf16[2,64,1280]{2,1,0:T(8,128)(2,1)} %param.19) | copy-start | bytes 983044
  34.3 0.8 copy-start.16
  34.4 1.3 copy-start.2
  34.4 442.3 %all-gather.2.cloned.1.call-start = ((), (), s32[]{:S(2)}) async-start(), calls=%async_computation | async-start | bytes 16588800 | tf_op jit(solution)/shard_map/all_gather | solution.py:105
  35.7 31.2 %copy-start.14 = (f32[1280]{0:T(1024)S(1)}, f32[1280]{0:T(1024)}, u32[]{:S(2)}) copy-start(f32[1280]{0:T(1024)} %param.16) | copy-start | bytes 15364
  35.7 31.3 %copy-start.15 = (f32[1280]{0:T(1024)S(1)}, f32[1280]{0:T(1024)}, u32[]{:S(2)}) copy-start(f32[1280]{0:T(1024)} %param.15) | copy-start | bytes 15364
  67.4 48.2 %collective-permute-start = (bf16[4,1,64,1280]{3,2,1,0:T(8,128)(2,1)S(1)}, bf16[4,1,64,1280]{3,2,1,0:T(8,128)(2,1)S(1)}, u32[]{:S(2)}, u32[]{:S(2)}) collective-permute-start(bf16[4,1,64,1280]{3,2,1,0:T(8,128)(2,1)S(1)} %multiply_convert_fusion), channel_id=1, source_target_pairs={{0,2},{2,4},{4,6},{6,8},{8,10},{10,12},{12,14},{1,3},{3,5},{5,7},{... | collective-permute-start | bytes 1966088 | tf_op jit(solution)/shard_map/ppermute | solution.py:22
  71.4 44.1 %collective-permute-start.1 = (bf16[4,1,64,1280]{3,2,1,0:T(8,128)(2,1)S(1)}, bf16[4,1,64,1280]{3,2,1,0:T(8,128)(2,1)S(1)}, u32[]{:S(2)}, u32[]{:S(2)}) collective-permute-start(bf16[4,1,64,1280]{3,2,1,0:T(8,128)(2,1)S(1)} %multiply_convert_fusion), channel_id=1, source_target_pairs={{2,0},{4,2},{6,4},{8,6},{10,8},{12,10},{14,12},{3,1},{5,3},{7,5},{... | collective-permute-start | bytes 1966088 | tf_op jit(solution)/shard_map/ppermute | solution.py:24
  116.3 11.0 %collective-permute-start.2 = (bf16[4,3,66,1280]{3,2,1,0:T(8,128)(2,1)S(1)}, bf16[4,3,66,1280]{3,2,1,0:T(8,128)(2,1)}, u32[]{:S(2)}, u32[]{:S(2)}) collective-permute-start(bf16[4,3,66,1280]{3,2,1,0:T(8,128)(2,1)S(1)} %fusion.5), channel_id=1, source_target_pairs={{0,1},{1,0},{2,3},{3,2},{4,5},{5,4},{6,7},{7,6},{8,9},{9,8},{10,11... | collective-permute-start | bytes 6082568 | tf_op jit(solution)/shard_map/ppermute | solution.py:32
  140.3 4.3 copy-start.3
  275.6 220.0 %copy-start.13 = (bf16[64,1280]{1,0:T(8,128)(2,1)S(1)}, bf16[64,1280]{1,0:T(8,128)(2,1)}, u32[]{:S(2)}) copy-start(bf16[64,1280]{1,0:T(8,128)(2,1)} %get-tuple-element.9) | copy-start | bytes 491524
  493.2 1.1 copy-start.9
  495.1 9.0 %collective-permute-start.3 = (f32[256,640]{1,0:T(8,128)}, f32[256,640]{1,0:T(8,128)}, u32[]{:S(2)}, u32[]{:S(2)}) collective-permute-start(f32[256,640]{1,0:T(8,128)} %slice.103), channel_id=1, source_target_pairs={{0,1},{1,0},{2,3},{3,2},{4,5},{5,4},{6,7},{7,6},{8,9},{9,8},{10,11... | collective-permute-start | bytes 1966088 | tf_op jit(solution)/shard_map/ppermute | solution.py:32
  495.6 3.3 copy-start.12
  498.9 2.9 copy-start.11
  501.9 2.2 copy-start.10
  505.3 1.3 copy-start.4
  505.3 1.4 copy-start.5
  505.3 1.4 copy-start.6
  505.3 1.5 copy-start.7
  505.4 2.7 copy-start.1
Sparse Core Ops, SparseCore 0:
  34.5 237.7 all-reduce.3
  274.5 202.1 all-gather.1
where the time goes:
time: 519 us; the launch traced here: 515 us
  waiting for transfers between devices  359 us (69%)
  between operations  31.9 us (6%)
  blocking collectives  30.1 us (6%)
  matrix products  28.6 us (6%)
  local copies, waits for them, and re-layouts  27.9 us (5%)
  other arithmetic  23.8 us (5%)
  starting transfers between devices  13.8 us (3%)
    all_gather x1, waiting for transfers between devices, shards(): lax.all_gather(kernel_weight, 'patch', axis=1, tiled=True)  201 us
    psum x1, waiting for transfers between devices, broadcast(): return lax.psum(block, axis)  111 us
    ppermute x1, waiting for transfers between devices, padded(): lax.ppermute(tail, axis, [(i, (i + 1) % count) for i in range(ends)])  41.8 us
    unnamed x46, local copies, waits for them, and re-layouts  19.1 us
    dot_general x1, matrix products, shards(): jnp.einsum('ptc,tco->po', taps, lax.all_gather(kernel_weight, 'patch', ax...  16.5 us
    psum x1, blocking collectives, shards(): squares = lax.psum(jnp.sum(centered * centered, axis=(1, 2, 4)), 'patch')  16.2 us
    psum x1, blocking collectives, shards(): totals = lax.psum(jnp.sum(grouped, axis=(1, 2, 4)), 'patch')  13.8 us
    dot_general x4, matrix products, shards(): deltas.append(jnp.dot(low, upper_limit, preferred_element_type=jnp.float32))  11.8 us
  transfers between devices with their start and end apart: 6, of which 4 were waited for; matrix products, arithmetic and copies ran while one was open for 8% of the time, Pallas kernels for 0%

commit v1 on v0

--- a/solution.py
+++ b/solution.py
@@ -1,9 +1,386 @@
+import functools
+
 import jax
 import jax.numpy as jnp
 from jax import lax
+from jax.experimental import pallas as pl
+from jax.experimental.pallas import tpu as pltpu
 from jax.sharding import PartitionSpec as P
 
 GROUPS = 32
+LANES = 128
+WIN = 256
+MESH = pl.DeviceIdType.MESH
+BF = jnp.bfloat16
+F32 = jnp.float32
+
+
+def hi_dot(a, b, dims):
+    return lax.dot_general(
+        a, b, (dims, ((), ())), precision=lax.Precision.HIGHEST, preferred_element_type=F32
+    )
+
+
+def block_kernel(
+    n, own, reqs, width, chans,
+    sel, hid, temb, gain, bias, w_hbm, d_hbm,
+    base_out, low_out,
+    act, acts_in, taps, wpad, dall, stat_out, stat_in,
+    xsend, xrecv, keep, zsend, zrecv, lsend, lrecv,
+    st_s, st_r, ac_s, ac_r, ac_l, d_s, d_r, d_l, w_s, w_r, w_l, dp_s, dp_r,
+    x_s, x_r, z_s, z_r, l_s, l_r,
+):
+    me = lax.axis_index("patch")
+    core = lax.axis_index("req")
+    mate = 1 - core
+    zs = n // 2
+    z, x = me // 2, me % 2
+    half = chans // 2
+    rank = dall.shape[1]
+    hrank = rank // 2
+    per = n and d_hbm.shape[0]
+
+    def window(j):
+        return pl.multiple_of((j * own) // LANES * LANES, LANES)
+
+    wpad[...] = jnp.zeros_like(wpad)
+
+    barrier = pltpu.get_barrier_semaphore()
+    for k in range(1, n):
+        pl.semaphore_signal(barrier, inc=1, device_id={"patch": (me + k) % n}, device_id_type=MESH)
+    pl.semaphore_signal(barrier, inc=1, device_id={"req": mate}, device_id_type=MESH)
+    pl.semaphore_wait(barrier, n)
+
+    inner = pl.multiple_of((me * own) % LANES, 32)
+
+    def w_dst(t, c):
+        return wpad.at[
+            t // 3,
+            pl.ds(pl.multiple_of((t % 3) * WIN + inner, 32), own),
+            pl.ds(pl.multiple_of(c * half, LANES), half),
+        ]
+
+    def w_remote(t, c):
+        return pltpu.make_async_remote_copy(
+            src_ref=w_hbm.at[t], dst_ref=w_dst(t, c), send_sem=w_s.at[t], recv_sem=w_r.at[t],
+            device_id={"req": mate}, device_id_type=MESH,
+        )
+
+    def w_local(t):
+        return pltpu.make_async_copy(w_hbm.at[t], w_dst(t, core), w_l.at[t])
+
+    for t in range(9):
+        w_local(t).start()
+        w_remote(t, core).start()
+
+    c_of = lax.broadcasted_iota(jnp.int32, (chans, LANES), 0)
+    g_of = lax.broadcasted_iota(jnp.int32, (chans, LANES), 1)
+    size = chans // GROUPS
+    member = jnp.where((c_of >= g_of * size) & (c_of < (g_of + 1) * size), 1.0, 0.0).astype(F32)
+    count = width * size
+    sums = [
+        jnp.sum(hid[r * width : (r + 1) * width, :] + temb[r : r + 1, :], axis=0, keepdims=True)
+        for r in range(reqs)
+    ]
+    pad = [jnp.zeros((8 - reqs, chans), F32)] if reqs < 8 else []
+    mean = hi_dot(jnp.concatenate(sums + pad, axis=0), member, ((1,), (0,))) / count
+    wide = hi_dot(mean, member, ((1,), (1,)))
+    squares = []
+    for r in range(reqs):
+        c = hid[r * width : (r + 1) * width, :] + temb[r : r + 1, :] - wide[r : r + 1, :]
+        squares.append(jnp.sum(c * c, axis=0, keepdims=True))
+    second = hi_dot(jnp.concatenate(squares + pad, axis=0), member, ((1,), (0,)))
+    stat_out[0] = mean
+    stat_out[1] = second
+
+    def st_copy(peer, src):
+        return pltpu.make_async_remote_copy(
+            src_ref=stat_out, dst_ref=stat_in.at[src], send_sem=st_s.at[peer], recv_sem=st_r.at[src],
+            device_id={"patch": peer}, device_id_type=MESH,
+        )
+
+    for k in range(1, n):
+        st_copy((me + k) % n, me).start()
+    stat_in[me] = stat_out[...]
+    for k in range(1, n):
+        st_copy((me + k) % n, (me + k) % n).wait_recv()
+    means = stat_in[:, 0]
+    total_mean = jnp.sum(means, axis=0) / n
+    spread = means - total_mean[None]
+    var = (jnp.sum(stat_in[:, 1], axis=0) + count * jnp.sum(spread * spread, axis=0)) / (count * n)
+    mean_w = hi_dot(total_mean, member, ((1,), (1,)))
+    inv_w = hi_dot(lax.rsqrt(var + 1e-05), member, ((1,), (1,)))
+    for r in range(reqs):
+        rows = slice(r * width, (r + 1) * width)
+        v = (hid[rows, :] + temb[r : r + 1, :] - mean_w[r : r + 1, :]) * inv_w[r : r + 1, :]
+        v = v * gain[...] + bias[...]
+        act[rows, :] = (v / (1.0 + jnp.exp(-v))).astype(BF)
+
+    def ac_copy(peer, src):
+        return pltpu.make_async_remote_copy(
+            src_ref=act.at[:, pl.ds(window(peer), WIN)], dst_ref=acts_in.at[src],
+            send_sem=ac_s.at[peer], recv_sem=ac_r.at[src],
+            device_id={"patch": peer}, device_id_type=MESH,
+        )
+
+    ac_own = pltpu.make_async_copy(act.at[:, pl.ds(window(me), WIN)], acts_in.at[me], ac_l)
+    for k in range(1, n):
+        ac_copy((me + k) % n, me).start()
+    ac_own.start()
+
+    rank_at = pl.multiple_of(core * hrank, hrank)
+
+    def d_src(t, peer):
+        return d_hbm.at[:, pl.ds(rank_at, hrank), pl.ds(pl.multiple_of(t * chans + window(peer), LANES), WIN)]
+
+    def d_dst(t, src):
+        return dall.at[pl.ds(src * per, per), pl.ds(rank_at, hrank), pl.ds(pl.multiple_of(t * WIN, WIN), WIN)]
+
+    def d_copy(t, peer, src):
+        return pltpu.make_async_remote_copy(
+            src_ref=d_src(t, peer), dst_ref=d_dst(t, src),
+            send_sem=d_s.at[peer, t], recv_sem=d_r.at[src, t],
+            device_id={"patch": peer}, device_id_type=MESH,
+        )
+
+    def d_own(t):
+        return pltpu.make_async_copy(d_src(t, me), d_dst(t, me), d_l.at[t])
+
+    @pl.loop(0, 9)
+    def _(t):
+        d_own(t).start()
+
+        @pl.loop(1, n)
+        def _(k):
+            d_copy(t, (me + k) % n, me).start()
+
+    taps[0] = jnp.zeros(taps.shape[1:], BF)
+    taps[n + 1] = jnp.zeros(taps.shape[1:], BF)
+    cells = reqs * width
+    px = lax.broadcasted_iota(jnp.int32, (cells, WIN), 0) % width
+    ch = lax.broadcasted_iota(jnp.int32, (cells, WIN), 1)
+    mine = (ch >= inner) & (ch < inner + own)
+
+    def lay(y):
+        v = jnp.where(mine, acts_in[y].astype(F32), 0.0)
+        taps[y + 1, :, 0:WIN] = jnp.where(px == 0, 0.0, pltpu.roll(v, 1, 0)).astype(BF)
+        taps[y + 1, :, WIN : 2 * WIN] = v.astype(BF)
+        taps[y + 1, :, 2 * WIN :] = jnp.where(px == width - 1, 0.0, pltpu.roll(v, cells - 1, 0)).astype(BF)
+
+    ac_own.wait()
+    lay(me)
+
+    @pl.loop(1, n)
+    def _(k):
+        y = (me + k) % n
+        ac_copy(y, y).wait_recv()
+        lay(y)
+
+    for t in range(9):
+        w_local(t).wait()
+        w_remote(t, mate).wait_recv()
+
+    def conv(y, put):
+        @pl.loop(0, chans // WIN)
+        def _(m):
+            cols = pl.ds(pl.multiple_of(m * WIN, WIN), WIN)
+            s = jnp.dot(taps[y], wpad[0, :, cols], preferred_element_type=F32)
+            s += jnp.dot(taps[y + 1], wpad[1, :, cols], preferred_element_type=F32)
+            s += jnp.dot(taps[y + 2], wpad[2, :, cols], preferred_element_type=F32)
+            put(cols, s)
+
+    def x_copy(i):
+        return pltpu.make_async_remote_copy(
+            src_ref=xsend.at[i], dst_ref=xrecv.at[i], send_sem=x_s.at[i], recv_sem=x_r.at[i],
+            device_id={"patch": me + 1 - 2 * x}, device_id_type=MESH,
+        )
+
+    def z_copy(i, zt, src):
+        return pltpu.make_async_remote_copy(
+            src_ref=zsend.at[i], dst_ref=zrecv.at[src], send_sem=z_s.at[i], recv_sem=z_r.at[src],
+            device_id={"patch": zt * 2 + x}, device_id_type=MESH,
+        )
+
+    def forward(i):
+        x_copy(i).wait_recv()
+        zsend[i] = (keep[...] + xrecv[i].astype(F32)).astype(BF)
+        z_copy(i, (z + 1 + i) % zs, z).start()
+
+    @pl.loop(0, zs)
+    def _(i):
+        zt = (z + 1 + i) % zs
+
+        def put_x(cols, s):
+            xsend[i, :, cols] = s.astype(BF)
+
+        conv(zt * 2 + 1 - x, put_x)
+        x_copy(i).start()
+
+        def put_keep(cols, s):
+            keep[:, cols] = s
+
+        conv(zt * 2 + x, put_keep)
+
+        @pl.when(i < zs - 1)
+        def _():
+            forward(i)
+
+    x_copy(zs - 1).wait_recv()
+    base_out[...] = keep[...] + xrecv[zs - 1].astype(F32)
+
+    @pl.loop(0, 9)
+    def _(t):
+        d_own(t).wait()
+
+        @pl.loop(1, n)
+        def _(k):
+            d_copy(t, (me + k) % n, (me + k) % n).wait_recv()
+
+    def dp_copy(at):
+        part = dall.at[:, pl.ds(pl.multiple_of(at * hrank, hrank), hrank), :]
+        return pltpu.make_async_remote_copy(
+            src_ref=part, dst_ref=part, send_sem=dp_s, recv_sem=dp_r,
+            device_id={"req": mate}, device_id_type=MESH,
+        )
+
+    dp_copy(core).start()
+    dp_copy(mate).wait_recv()
+    for r in range(reqs):
+        factor = dall[sel[r]]
+        low = jnp.zeros((n * width, rank), F32)
+        for dy in range(3):
+            lhs = taps[dy : dy + n, r * width : (r + 1) * width, :].reshape(n * width, 3 * WIN)
+            low += lax.dot_general(
+                lhs, factor[:, dy * 3 * WIN : (dy + 1) * 3 * WIN], (((1,), (1,)), ((), ())),
+                preferred_element_type=F32,
+            )
+        high = low.astype(BF).astype(F32)
+        both = jnp.concatenate([high, low - high], axis=1).astype(BF)
+        lsend[:, r * width : (r + 1) * width, :] = both.reshape(n, width, 2 * rank)
+
+    def l_copy(peer, src):
+        return pltpu.make_async_remote_copy(
+            src_ref=lsend.at[peer], dst_ref=lrecv.at[src], send_sem=l_s.at[peer], recv_sem=l_r.at[src],
+            device_id={"patch": peer}, device_id_type=MESH,
+        )
+
+    for k in range(1, n):
+        l_copy((me + k) % n, me).start()
+
+    @pl.loop(1, zs)
+    def _(k):
+        src = (z + k) % zs
+        z_copy(0, src, src).wait_recv()
+        base_out[...] += zrecv[src].astype(F32)
+
+    both = lsend[me].astype(F32)
+    for k in range(1, n):
+        src = (me + k) % n
+        l_copy(src, src).wait_recv()
+        both += lrecv[src].astype(F32)
+    low_out[...] = (both[:, :rank] + both[:, rank:]).astype(BF)
+
+    dp_copy(core).wait_send()
+    for t in range(9):
+        w_remote(t, core).wait_send()
+    for k in range(1, n):
+        st_copy((me + k) % n, me).wait_send()
+        ac_copy((me + k) % n, me).wait_send()
+        l_copy((me + k) % n, me).wait_send()
+
+    @pl.loop(0, 9)
+    def _(t):
+        @pl.loop(1, n)
+        def _(k):
+            d_copy(t, (me + k) % n, me).wait_send()
+
+    @pl.loop(0, zs)
+    def _(i):
+        x_copy(i).wait_send()
+
+    @pl.loop(0, zs - 1)
+    def _(i):
+        z_copy(i, (z + 1 + i) % zs, z).wait_send()
+
+
+def conv_and_low(n, sel, hid, temb, gain, bias, weight, down):
+    cells, chans = hid.shape
+    reqs = sel.shape[0]
+    width = cells // reqs
+    own = weight.shape[1]
+    per, rank, _ = down.shape
+    zs = n // 2
+    dma = pltpu.SemaphoreType.DMA
+    vmem = pl.BlockSpec(memory_space=pltpu.VMEM)
+    hbm = pl.BlockSpec(memory_space=pl.ANY)
+    return pl.pallas_call(
+        functools.partial(block_kernel, n, own, reqs, width, chans),
+        out_shape=(
+            jax.ShapeDtypeStruct((cells, chans), F32),
+            jax.ShapeDtypeStruct((cells, rank), BF),
+        ),
+        in_specs=[pl.BlockSpec(memory_space=pltpu.SMEM), vmem, vmem, vmem, vmem, hbm, hbm],
+        out_specs=(vmem, vmem),
+        scratch_shapes=[
+            pltpu.VMEM((cells, chans), BF),
+            pltpu.VMEM((n, cells, WIN), BF),
+            pltpu.VMEM((n + 2, cells, 3 * WIN), BF),
+            pltpu.VMEM((3, 3 * WIN, chans), BF),
+            pltpu.VMEM((n * per, rank, 9 * WIN), BF),
+            pltpu.VMEM((2, 8, LANES), F32),
+            pltpu.VMEM((n, 2, 8, LANES), F32),
+            pltpu.VMEM((zs, cells, chans), BF),
+            pltpu.VMEM((zs, cells, chans), BF),
+            pltpu.VMEM((cells, chans), F32),
+            pltpu.VMEM((zs - 1, cells, chans), BF),
+            pltpu.VMEM((zs, cells, chans), BF),
+            pltpu.VMEM((n, cells, 2 * rank), BF),
+            pltpu.VMEM((n, cells, 2 * rank), BF),
+            dma((n,)), dma((n,)),
+            dma((n,)), dma((n,)), dma,
+            dma((n, 9)), dma((n, 9)), dma((9,)),
+            dma((9,)), dma((9,)), dma((9,)),
+            dma, dma,
+            dma((zs,)), dma((zs,)),
+            dma((zs - 1,)), dma((zs,)),
+            dma((n,)), dma((n,)),
+        ],
+        compiler_params=pltpu.CompilerParams(
+            collective_id=0, has_side_effects=True, vmem_limit_bytes=56 * 2**20
+        ),
+        cost_estimate=pl.CostEstimate(
+            flops=2 * n * cells * 9 * WIN * chans, bytes_accessed=10**8, transcendentals=0
+        ),
+    )(sel, hid, temb, gain, bias, weight, down)
+
+
+def split_contraction(
+    hidden, skip, timestep_embedding_table, timesteps, group_norm_gain, group_norm_bias,
+    kernel_weight, adapter_down_weight, adapter_up_weight, request_adapter, adapter_row_table,
+):
+    n = lax.axis_size("patch")
+    reqs, rows, width, chans = hidden.shape
+    per = adapter_up_weight.shape[0]
+    sel = adapter_row_table[request_adapter]
+    temb = timestep_embedding_table[timesteps]
+    spot = jnp.clip(sel - lax.axis_index("patch") * per, 0, per - 1)
+    here = (sel // per == lax.axis_index("patch"))[:, None, None]
+    up = lax.psum(jnp.where(here, adapter_up_weight[spot], jnp.zeros((), BF)), "patch")
+    base, low = conv_and_low(
+        n, sel, hidden.reshape(reqs * width, chans), temb, group_norm_gain[None],
+        group_norm_bias[None], kernel_weight, adapter_down_weight,
+    )
+    delta = jnp.einsum("rpk,rkc->rpc", low.reshape(reqs, width, -1), up, preferred_element_type=F32)
+    return skip + (base.reshape(reqs, width, chans) + delta).reshape(hidden.shape)
+
+
+def fits(n, hidden, kernel_weight, down):
+    own = kernel_weight.shape[1]
+    ends = all(j * own // LANES * LANES + WIN <= hidden.shape[3] and j * own % LANES + own <= WIN for j in range(n))
+    return (
+        n % 2 == 0 and n <= 8 and hidden.shape[1] == 1 and hidden.shape[0] <= 8
+        and own % 32 == 0 and ends and down.shape[1] == 64
+    )
 
 
 def broadcast(block, axis, owner):
@@ -132,8 +509,14 @@
 
 
 def solution(mesh):
+    def step(*args):
+        n = lax.axis_size("patch")
+        if fits(n, args[0], args[6], args[7]):
+            return split_contraction(*args)
+        return shards(*args)
+
     return jax.shard_map(
-        shards,
+        step,
         mesh=mesh,
         in_specs=(
             P(("groups", "req"), "patch", None, None),

time: 519 us -> 195 us (0.38)
  waiting for transfers between devices: 359 us -> 0.04 us
  Pallas kernels: 0 us -> 171 us
  blocking collectives: 30.1 us -> 0 us
  matrix products: 28.6 us -> 2.91 us
  local copies, waits for them, and re-layouts: 27.9 us -> 4.28 us
  other arithmetic: 23.8 us -> 1.7 us
  between operations: 31.9 us -> 13.5 us
  starting transfers between devices: 13.8 us -> 0.01 us
    all_gather x1 -> x0, waiting for transfers between devices: 201 us -> none  [shards(): lax.all_gather(kernel_weight, 'patch', axis=1, tiled=True)]
    pallas_call x0 -> x1, Pallas kernels: none -> 171 us  [conv_and_low(): pl.pallas_call(functools.partial(block_kernel, n, own, reqs, width, chans...]
    psum x1, waiting for transfers between devices: 111 us -> 0.02 us  [split_contraction(): lax.psum(jnp.where(here, adapter_up_weight[spot], jnp.zeros((), BF)), 'pa...]
    ppermute x4 -> x0, waiting for transfers between devices: 45.9 us -> none  [the longest x1 41.8 us: padded(): lax.ppermute(tail, axis, [(i, (i + 1) % count) for i in range(ends)])]
    psum x2 -> x0, blocking collectives: 30.1 us -> none  [the longest x1 16.2 us: shards(): squares = lax.psum(jnp.sum(centered * centered, axis=(1, 2, 4)), 'patch')]
    dot_general x6 -> x1, matrix products: 28.6 us -> 2.91 us  [split_contraction(): jnp.einsum('rpk,rkc->rpc', low.reshape(reqs, width, -1), up, preferred_el...]
    unnamed x46 -> x14, local copies, waits for them, and re-layouts: 19.1 us -> 0.04 us
    ppermute x4 -> x0, starting transfers between devices: 13.8 us -> none  [the longest x2 7.42 us: from_partner(): lax.ppermute(x, axis, [(i, i ^ 1 << stride) for i in range(lax.axis_size(...]
  transfers between devices with their start and end apart: 6 -> 1, of which waited for: 4 -> 0; matrix products, arithmetic and copies ran while one was open for 8% -> 1% of each run, Pallas kernels for 0% -> 88%
where the time goes in v1:
time: 195 us; the launch traced here: 193 us
  Pallas kernels  171 us (88%)
  between operations  13.5 us (7%)
  local copies, waits for them, and re-layouts  4.28 us (2%)
  matrix products  2.91 us (1%)
    pallas_call x1, Pallas kernels, conv_and_low(): pl.pallas_call(functools.partial(block_kernel, n, own, reqs, width, chans...  171 us
  transfers between devices with their start and end apart: 1, of which 0 were waited for; matrix products, arithmetic and copies ran while one was open for 1% of the time, Pallas kernels for 88%

profile of v1, /device:TPU:25, one launch (start us, length us, event | category | flops | bytes accessed | tf_op | source)
XLA Modules:
  0.0 193.4 jit_solution(294176000708954268)
XLA Ops:
  6.5 0.0 copy-start
  6.5 0.0 all-reduce.2.cloned.1.call-start
  6.5 0.7 compare_select_fusion.2
  7.3 1.3 gather_fusion
  8.5 0.0 copy-start.5
  8.6 0.0 copy-done
  8.6 0.6 gather_fusion.2
  9.2 0.0 copy-start.6
  9.2 0.0 copy-start.3
  9.2 0.0 copy-start.4
  9.2 0.0 copy-start.2
  9.2 1.0 broadcast_select_fusion
  10.2 0.0 copy-done.5
  10.2 0.0 all-reduce.2.cloned.1.call-update
  10.2 0.0 copy-done.6
  10.3 0.0 copy-done.3
  10.3 0.6 broadcast_in_dim.28.gain
  10.9 0.0 copy-done.4
  10.9 0.6 broadcast_in_dim.29.bias
  11.5 0.0 copy-done.2
  11.5 1.2 gather_fusion.1
  12.6 0.0 copy-start.1
  12.6 170.9 %shard_map.109 = (f32[256,1280]{1,0:T(8,128)}, bf16[256,64]{1,0:T(8,128)(2,1)}) custom-call(s32[4]{0:T(128)} %copy-done.5, f32[256,1280]{1,0:T(8,128)} %bitcast.21, f32[4,1280]{1,0:T(4,128)} %gather_fusion.1, f32[1,1280]{1,0:T(1,128)} %broadcast_in_dim.28.gain, f32[1,1280]{1,0:T(1,128)} %broadcast_in_dim.29.bias, bf16[9,160,640]{2,1,0:T(8,128)(2,1)} %w_hbm.1, ...), custom_call_target="tpu_custom_call" | custom-call | flops 12079595520 | bytes 100000000 | tf_op jit(solution)/shard_map/pallas_call | solution.py:316
  183.6 0.0 all-reduce.2.cloned.1.call-done
  183.6 0.0 copy-done.1
  183.6 2.9 %fusion.2 = f32[4,1,64,1280]{3,2,1,0:T(8,128)} fusion(f32[4,64,1280]{2,1,0:T(8,128)} %bitcast.19, bf16[4,64,64]{2,1,0:T(8,128)(2,1)} %bitcast.20, bf16[4,64,1280]{2,1,0:T(8,128)(2,1)} %all-reduce.2.cloned.1.call-done, f32[4,1,64,1280]{3,2,1,0:T(8,128)S(1)} %copy-done.1), kind=kOutput, calls=%fused_computation.6 | convolution fusion | flops 42598400 | bytes 4620288 | tf_op jit(solution)/shard_map/rpk,rkc->rpc/dot_general | solution.py:373
  (6 shorter events, 0.0 us)
Async XLA Ops:
  6.5 2.1 %copy-start = (bf16[2,64,1280]{2,1,0:T(8,128)(2,1)S(1)}, bf16[2,64,1280]{2,1,0:T(8,128)(2,1)}, u32[]{:S(2)}) copy-start(bf16[2,64,1280]{2,1,0:T(8,128)(2,1)} %param.19) | copy-start | bytes 983044
  6.5 177.1 %all-reduce.2.cloned.1.call-start = ((), (), s32[]{:S(2)}) async-start(), calls=%async_computation | async-start | bytes 1310720 | tf_op jit(solution)/shard_map/psum | solution.py:368
  8.5 1.7 copy-start.5
  9.2 1.0 copy-start.6
  9.2 1.1 copy-start.3
  9.2 1.6 copy-start.4
  9.2 2.2 %copy-start.2 = (f32[50,1280]{1,0:T(8,128)S(1)}, f32[50,1280]{1,0:T(8,128)}, u32[]{:S(2)}) copy-start(f32[50,1280]{1,0:T(8,128)} %param.13) | copy-start | bytes 768004
  12.6 171.0 %copy-start.1 = (f32[4,1,64,1280]{3,2,1,0:T(8,128)S(1)}, f32[4,1,64,1280]{3,2,1,0:T(8,128)}, u32[]{:S(2)}) copy-start(f32[4,1,64,1280]{3,2,1,0:T(8,128)} %param.12) | copy-start | bytes 3932164
Sparse Core Ops, SparseCore 0:
  10.8 96.3 all-reduce.1

commit v2 on v1

--- a/solution.py
+++ b/solution.py
@@ -23,12 +23,12 @@
 
 def block_kernel(
     n, own, reqs, width, chans,
-    sel, hid, temb, gain, bias, w_hbm, d_hbm,
-    base_out, low_out,
-    act, acts_in, taps, wpad, dall, stat_out, stat_in,
+    steps, asked, row_of, hid, skip, table, gain, bias, w_hbm, d_hbm, u_hbm,
+    out,
+    act, acts_in, taps, wpad, dall, uall, stat_out, stat_in,
     xsend, xrecv, keep, zsend, zrecv, lsend, lrecv,
     st_s, st_r, ac_s, ac_r, ac_l, d_s, d_r, d_l, w_s, w_r, w_l, dp_s, dp_r,
-    x_s, x_r, z_s, z_r, l_s, l_r,
+    x_s, x_r, z_s, z_r, l_s, l_r, u_s, u_f, u_r, u_l, up_s, up_r,
 ):
     me = lax.axis_index("patch")
     core = lax.axis_index("req")
@@ -38,7 +38,9 @@
     half = chans // 2
     rank = dall.shape[1]
     hrank = rank // 2
-    per = n and d_hbm.shape[0]
+    per = d_hbm.shape[0]
+    temb = [table[pl.ds(steps[r], 1), :] for r in range(reqs)]
+    sel = [row_of[asked[r]] for r in range(reqs)]
 
     def window(j):
         return pl.multiple_of((j * own) // LANES * LANES, LANES)
@@ -73,13 +75,68 @@
         w_local(t).start()
         w_remote(t, core).start()
 
+    rank_at = pl.multiple_of(core * hrank, hrank)
+
+    def d_src(t, peer):
+        return d_hbm.at[:, pl.ds(rank_at, hrank), pl.ds(pl.multiple_of(t * chans + window(peer), LANES), WIN)]
+
+    def d_dst(t, src):
+        return dall.at[pl.ds(src * per, per), pl.ds(rank_at, hrank), pl.ds(pl.multiple_of(t * WIN, WIN), WIN)]
+
+    def d_copy(t, peer, src):
+        return pltpu.make_async_remote_copy(
+            src_ref=d_src(t, peer), dst_ref=d_dst(t, src),
+            send_sem=d_s.at[peer, t], recv_sem=d_r.at[src, t],
+            device_id={"patch": peer}, device_id_type=MESH,
+        )
+
+    def d_own(t):
+        return pltpu.make_async_copy(d_src(t, me), d_dst(t, me), d_l.at[t])
+
+    def send_down(lo, hi):
+        @pl.loop(lo, hi)
+        def _(t):
+            d_own(t).start()
+
+            @pl.loop(1, n)
+            def _(k):
+                d_copy(t, (me + k) % n, me).start()
+
+    def u_dst(src):
+        return uall.at[pl.ds(src * per, per), pl.ds(rank_at, hrank), :]
+
+    near = me + 1 - 2 * x
+
+    def u_copy(peer, src):
+        return pltpu.make_async_remote_copy(
+            src_ref=u_hbm.at[:, pl.ds(rank_at, hrank), :], dst_ref=u_dst(src),
+            send_sem=u_s.at[peer], recv_sem=u_r.at[src],
+            device_id={"patch": peer}, device_id_type=MESH,
+        )
+
+    def u_pass(src):
+        return pltpu.make_async_remote_copy(
+            src_ref=u_dst(src), dst_ref=u_dst(src), send_sem=u_f.at[src], recv_sem=u_r.at[src],
+            device_id={"patch": near}, device_id_type=MESH,
+        )
+
+    u_own = pltpu.make_async_copy(u_hbm.at[:, pl.ds(rank_at, hrank), :], u_dst(me), u_l)
+
+    def send_up():
+        u_own.start()
+        u_copy(near, me).start()
+        for k in range(1, zs):
+            u_copy((z + k) % zs * 2 + x, me).start()
+
+    send_down(0, 3)
+
     c_of = lax.broadcasted_iota(jnp.int32, (chans, LANES), 0)
     g_of = lax.broadcasted_iota(jnp.int32, (chans, LANES), 1)
     size = chans // GROUPS
     member = jnp.where((c_of >= g_of * size) & (c_of < (g_of + 1) * size), 1.0, 0.0).astype(F32)
     count = width * size
     sums = [
-        jnp.sum(hid[r * width : (r + 1) * width, :] + temb[r : r + 1, :], axis=0, keepdims=True)
+        jnp.sum(hid[r * width : (r + 1) * width, :] + temb[r], axis=0, keepdims=True)
         for r in range(reqs)
     ]
     pad = [jnp.zeros((8 - reqs, chans), F32)] if reqs < 8 else []
@@ -87,7 +144,7 @@
     wide = hi_dot(mean, member, ((1,), (1,)))
     squares = []
     for r in range(reqs):
-        c = hid[r * width : (r + 1) * width, :] + temb[r : r + 1, :] - wide[r : r + 1, :]
+        c = hid[r * width : (r + 1) * width, :] + temb[r] - wide[r : r + 1, :]
         squares.append(jnp.sum(c * c, axis=0, keepdims=True))
     second = hi_dot(jnp.concatenate(squares + pad, axis=0), member, ((1,), (0,)))
     stat_out[0] = mean
@@ -112,7 +169,7 @@
     inv_w = hi_dot(lax.rsqrt(var + 1e-05), member, ((1,), (1,)))
     for r in range(reqs):
         rows = slice(r * width, (r + 1) * width)
-        v = (hid[rows, :] + temb[r : r + 1, :] - mean_w[r : r + 1, :]) * inv_w[r : r + 1, :]
+        v = (hid[rows, :] + temb[r] - mean_w[r : r + 1, :]) * inv_w[r : r + 1, :]
         v = v * gain[...] + bias[...]
         act[rows, :] = (v / (1.0 + jnp.exp(-v))).astype(BF)
 
@@ -128,31 +185,8 @@
         ac_copy((me + k) % n, me).start()
     ac_own.start()
 
-    rank_at = pl.multiple_of(core * hrank, hrank)
-
-    def d_src(t, peer):
-        return d_hbm.at[:, pl.ds(rank_at, hrank), pl.ds(pl.multiple_of(t * chans + window(peer), LANES), WIN)]
-
-    def d_dst(t, src):
-        return dall.at[pl.ds(src * per, per), pl.ds(rank_at, hrank), pl.ds(pl.multiple_of(t * WIN, WIN), WIN)]
-
-    def d_copy(t, peer, src):
-        return pltpu.make_async_remote_copy(
-            src_ref=d_src(t, peer), dst_ref=d_dst(t, src),
-            send_sem=d_s.at[peer, t], recv_sem=d_r.at[src, t],
-            device_id={"patch": peer}, device_id_type=MESH,
-        )
-
-    def d_own(t):
-        return pltpu.make_async_copy(d_src(t, me), d_dst(t, me), d_l.at[t])
-
-    @pl.loop(0, 9)
-    def _(t):
-        d_own(t).start()
-
-        @pl.loop(1, n)
-        def _(k):
-            d_copy(t, (me + k) % n, me).start()
+    send_down(3, 9)
+    send_up()
 
     taps[0] = jnp.zeros(taps.shape[1:], BF)
     taps[n + 1] = jnp.zeros(taps.shape[1:], BF)
@@ -192,7 +226,7 @@
     def x_copy(i):
         return pltpu.make_async_remote_copy(
             src_ref=xsend.at[i], dst_ref=xrecv.at[i], send_sem=x_s.at[i], recv_sem=x_r.at[i],
-            device_id={"patch": me + 1 - 2 * x}, device_id_type=MESH,
+            device_id={"patch": near}, device_id_type=MESH,
         )
 
     def z_copy(i, zt, src):
@@ -203,30 +237,25 @@
 
     def forward(i):
         x_copy(i).wait_recv()
-        zsend[i] = (keep[...] + xrecv[i].astype(F32)).astype(BF)
+        zsend[i] = (keep[i] + xrecv[i].astype(F32)).astype(BF)
         z_copy(i, (z + 1 + i) % zs, z).start()
 
     @pl.loop(0, zs)
     def _(i):
-        zt = (z + 1 + i) % zs
-
-        def put_x(cols, s):
+        def put(cols, s):
             xsend[i, :, cols] = s.astype(BF)
 
-        conv(zt * 2 + 1 - x, put_x)
+        conv((z + 1 + i) % zs * 2 + 1 - x, put)
         x_copy(i).start()
 
-        def put_keep(cols, s):
-            keep[:, cols] = s
-
-        conv(zt * 2 + x, put_keep)
-
-        @pl.when(i < zs - 1)
-        def _():
-            forward(i)
-
-    x_copy(zs - 1).wait_recv()
-    base_out[...] = keep[...] + xrecv[zs - 1].astype(F32)
+    @pl.loop(0, zs)
+    def _(i):
+        def put(cols, s):
+            keep[i, :, cols] = s
+
+        conv((z + 1 + i) % zs * 2 + x, put)
+
+    forward(0)
 
     @pl.loop(0, 9)
     def _(t):
@@ -244,19 +273,27 @@
         )
 
     dp_copy(core).start()
+    for k in range(1, zs):
+        src = (z + k) % zs * 2 + x
+        u_copy(src, src).wait_recv()
+        u_pass(src).start()
+    for i in range(1, zs - 1):
+        forward(i)
     dp_copy(mate).wait_recv()
-    for r in range(reqs):
-        factor = dall[sel[r]]
-        low = jnp.zeros((n * width, rank), F32)
-        for dy in range(3):
-            lhs = taps[dy : dy + n, r * width : (r + 1) * width, :].reshape(n * width, 3 * WIN)
-            low += lax.dot_general(
-                lhs, factor[:, dy * 3 * WIN : (dy + 1) * 3 * WIN], (((1,), (1,)), ((), ())),
-                preferred_element_type=F32,
-            )
-        high = low.astype(BF).astype(F32)
-        both = jnp.concatenate([high, low - high], axis=1).astype(BF)
-        lsend[:, r * width : (r + 1) * width, :] = both.reshape(n, width, 2 * rank)
+    for q in range(reqs // 2):
+        pair = []
+        for r in (2 * q, 2 * q + 1):
+            factor = dall[sel[r]]
+            low = jnp.zeros((n * width, rank), F32)
+            for dy in range(3):
+                lhs = taps[dy : dy + n, r * width : (r + 1) * width, :].reshape(n * width, 3 * WIN)
+                low += lax.dot_general(
+                    lhs, factor[:, dy * 3 * WIN : (dy + 1) * 3 * WIN], (((1,), (1,)), ((), ())),
+                    preferred_element_type=F32,
+                )
+            pair.append(low)
+        both = jnp.concatenate(pair, axis=1).astype(BF)
+        lsend[:, q * width : (q + 1) * width, :] = both.reshape(n, width, 2 * rank)
 
     def l_copy(peer, src):
         return pltpu.make_async_remote_copy(
@@ -267,20 +304,42 @@
     for k in range(1, n):
         l_copy((me + k) % n, me).start()
 
-    @pl.loop(1, zs)
-    def _(k):
+    u_own.wait()
+    u_copy(near, near).wait_recv()
+    for k in range(1, zs):
+        u_pass((z + k) % zs * 2 + 1 - x).wait_recv()
+
+    def up_copy(at):
+        part = uall.at[:, pl.ds(pl.multiple_of(at * hrank, hrank), hrank), :]
+        return pltpu.make_async_remote_copy(
+            src_ref=part, dst_ref=part, send_sem=up_s, recv_sem=up_r,
+            device_id={"req": mate}, device_id_type=MESH,
+        )
+
+    up_copy(core).start()
+    x_copy(zs - 1).wait_recv()
+    out[...] = skip[...] + keep[zs - 1] + xrecv[zs - 1].astype(F32)
+    for k in range(1, zs):
         src = (z + k) % zs
         z_copy(0, src, src).wait_recv()
-        base_out[...] += zrecv[src].astype(F32)
-
+        out[...] += zrecv[src].astype(F32)
+    up_copy(mate).wait_recv()
     both = lsend[me].astype(F32)
     for k in range(1, n):
         src = (me + k) % n
         l_copy(src, src).wait_recv()
         both += lrecv[src].astype(F32)
-    low_out[...] = (both[:, :rank] + both[:, rank:]).astype(BF)
+    both = both.astype(BF)
+    for r in range(reqs):
+        low = both[r // 2 * width : (r // 2 + 1) * width, r % 2 * rank : (r % 2 + 1) * rank]
+        out[r * width : (r + 1) * width, :] += jnp.dot(low, uall[sel[r]], preferred_element_type=F32)
 
     dp_copy(core).wait_send()
+    up_copy(core).wait_send()
+    u_copy(near, me).wait_send()
+    for k in range(1, zs):
+        u_copy((z + k) % zs * 2 + x, me).wait_send()
+        u_pass((z + k) % zs * 2 + x).wait_send()
     for t in range(9):
         w_remote(t, core).wait_send()
     for k in range(1, n):
@@ -303,9 +362,9 @@
         z_copy(i, (z + 1 + i) % zs, z).wait_send()
 
 
-def conv_and_low(n, sel, hid, temb, gain, bias, weight, down):
+def run_block(n, steps, asked, row_of, hid, skip, table, gain, bias, weight, down, up):
     cells, chans = hid.shape
-    reqs = sel.shape[0]
+    reqs = asked.shape[0]
     width = cells // reqs
     own = weight.shape[1]
     per, rank, _ = down.shape
@@ -313,29 +372,28 @@
     dma = pltpu.SemaphoreType.DMA
     vmem = pl.BlockSpec(memory_space=pltpu.VMEM)
     hbm = pl.BlockSpec(memory_space=pl.ANY)
+    smem = pl.BlockSpec(memory_space=pltpu.SMEM)
     return pl.pallas_call(
         functools.partial(block_kernel, n, own, reqs, width, chans),
-        out_shape=(
-            jax.ShapeDtypeStruct((cells, chans), F32),
-            jax.ShapeDtypeStruct((cells, rank), BF),
-        ),
-        in_specs=[pl.BlockSpec(memory_space=pltpu.SMEM), vmem, vmem, vmem, vmem, hbm, hbm],
-        out_specs=(vmem, vmem),
+        out_shape=jax.ShapeDtypeStruct((cells, chans), F32),
+        in_specs=[smem] * 3 + [vmem] * 5 + [hbm] * 3,
+        out_specs=vmem,
         scratch_shapes=[
             pltpu.VMEM((cells, chans), BF),
             pltpu.VMEM((n, cells, WIN), BF),
             pltpu.VMEM((n + 2, cells, 3 * WIN), BF),
             pltpu.VMEM((3, 3 * WIN, chans), BF),
             pltpu.VMEM((n * per, rank, 9 * WIN), BF),
+            pltpu.VMEM((n * per, rank, chans), BF),
             pltpu.VMEM((2, 8, LANES), F32),
             pltpu.VMEM((n, 2, 8, LANES), F32),
             pltpu.VMEM((zs, cells, chans), BF),
             pltpu.VMEM((zs, cells, chans), BF),
-            pltpu.VMEM((cells, chans), F32),
+            pltpu.VMEM((zs, cells, chans), F32),
             pltpu.VMEM((zs - 1, cells, chans), BF),
             pltpu.VMEM((zs, cells, chans), BF),
-            pltpu.VMEM((n, cells, 2 * rank), BF),
-            pltpu.VMEM((n, cells, 2 * rank), BF),
+            pltpu.VMEM((n, cells // 2, 2 * rank), BF),
+            pltpu.VMEM((n, cells // 2, 2 * rank), BF),
             dma((n,)), dma((n,)),
             dma((n,)), dma((n,)), dma,
             dma((n, 9)), dma((n, 9)), dma((9,)),
@@ -344,6 +402,8 @@
             dma((zs,)), dma((zs,)),
             dma((zs - 1,)), dma((zs,)),
             dma((n,)), dma((n,)),
+            dma((n,)), dma((n,)), dma((n,)), dma,
+            dma, dma,
         ],
         compiler_params=pltpu.CompilerParams(
             collective_id=0, has_side_effects=True, vmem_limit_bytes=56 * 2**20
@@ -351,34 +411,28 @@
         cost_estimate=pl.CostEstimate(
             flops=2 * n * cells * 9 * WIN * chans, bytes_accessed=10**8, transcendentals=0
         ),
-    )(sel, hid, temb, gain, bias, weight, down)
+    )(steps, asked, row_of, hid, skip, table, gain, bias, weight, down, up)
 
 
 def split_contraction(
     hidden, skip, timestep_embedding_table, timesteps, group_norm_gain, group_norm_bias,
     kernel_weight, adapter_down_weight, adapter_up_weight, request_adapter, adapter_row_table,
 ):
-    n = lax.axis_size("patch")
-    reqs, rows, width, chans = hidden.shape
-    per = adapter_up_weight.shape[0]
-    sel = adapter_row_table[request_adapter]
-    temb = timestep_embedding_table[timesteps]
-    spot = jnp.clip(sel - lax.axis_index("patch") * per, 0, per - 1)
-    here = (sel // per == lax.axis_index("patch"))[:, None, None]
-    up = lax.psum(jnp.where(here, adapter_up_weight[spot], jnp.zeros((), BF)), "patch")
-    base, low = conv_and_low(
-        n, sel, hidden.reshape(reqs * width, chans), temb, group_norm_gain[None],
-        group_norm_bias[None], kernel_weight, adapter_down_weight,
-    )
-    delta = jnp.einsum("rpk,rkc->rpc", low.reshape(reqs, width, -1), up, preferred_element_type=F32)
-    return skip + (base.reshape(reqs, width, chans) + delta).reshape(hidden.shape)
+    shape = hidden.shape
+    flat = (shape[0] * shape[1] * shape[2], shape[3])
+    return run_block(
+        lax.axis_size("patch"), timesteps, request_adapter, adapter_row_table,
+        hidden.reshape(flat), skip.reshape(flat), timestep_embedding_table,
+        group_norm_gain[None], group_norm_bias[None],
+        kernel_weight, adapter_down_weight, adapter_up_weight,
+    ).reshape(shape)
 
 
 def fits(n, hidden, kernel_weight, down):
     own = kernel_weight.shape[1]
     ends = all(j * own // LANES * LANES + WIN <= hidden.shape[3] and j * own % LANES + own <= WIN for j in range(n))
     return (
-        n % 2 == 0 and n <= 8 and hidden.shape[1] == 1 and hidden.shape[0] <= 8
+        n % 2 == 0 and n <= 8 and hidden.shape[1] == 1 and hidden.shape[0] in (2, 4, 6, 8)
         and own % 32 == 0 and ends and down.shape[1] == 64
     )
 

time: 195 us -> 182 us (0.933)
  between operations: 13.5 us -> 0.01 us
  Pallas kernels: 171 us -> 177 us
  matrix products: 2.91 us -> 0 us
    pallas_call x1, Pallas kernels: 171 us -> 177 us  [run_block(): pl.pallas_call(functools.partial(block_kernel, n, own, reqs, width, chans...]
    gather x3 -> x0, local copies, waits for them, and re-layouts: 3.05 us -> none  [the longest x1 1.29 us: split_contraction(): sel = adapter_row_table[request_adapter]]
    dot_general x1 -> x0, matrix products: 2.91 us -> none  [split_contraction(): jnp.einsum('rpk,rkc->rpc', low.reshape(reqs, width, -1), up, preferred_el...]
    unnamed x14 -> x1, local copies, waits for them, and re-layouts: 0.04 us -> 2.5 us
  transfers between devices with their start and end apart: 1 -> 0, of which waited for: 0 -> 0; matrix products, arithmetic and copies ran while one was open for 1% -> 0% of each run, Pallas kernels for 88% -> 0%
where the time goes in v2:
time: 182 us
  Pallas kernels  177 us (97%)
  local copies, waits for them, and re-layouts  5.08 us (3%)
    pallas_call x1, Pallas kernels, run_block(): pl.pallas_call(functools.partial(block_kernel, n, own, reqs, width, chans...  177 us

profile of v2, /device:TPU:25, one launch (start us, length us, event | category | flops | bytes accessed | tf_op | source)
XLA Modules:
  0.0 181.8 jit_solution(11822872415231030942)
XLA Ops:
  0.0 1.3 broadcast_in_dim.6.gain
  1.3 1.3 broadcast_in_dim.7.bias
  2.6 176.7 %shard_map.109 = f32[256,1280]{1,0:T(8,128)} custom-call(s32[4]{0:T(128)} %steps.1, s32[4]{0:T(128)} %asked.1, s32[16]{0:T(128)} %row_of.1, f32[256,1280]{1,0:T(8,128)} %bitcast.6, f32[256,1280]{1,0:T(8,128)} %bitcast.7, f32[50,1280]{1,0:T(8,128)} %table.1, f32[1,1280]{1,0:T(1,128)} %broadcast_in_dim.6.gain, f32[1,1280]{1,0:T(1,128)} %broadcast_in_dim.7.bias, ...), custom_call_target="tpu_custom_call" | custom-call | flops 12079595520 | bytes 100000000 | tf_op jit(solution)/shard_map/pallas_call | solution.py:376
  179.3 2.5 %copy.14 = f32[4,1,64,1280]{3,2,1,0:T(8,128)} copy(f32[4,1,64,1280]{3,2,1,0:T(8,128)} %bitcast.5) | data formatting | bytes 2621440

commit v3 on v2

--- a/solution.py
+++ b/solution.py
@@ -229,33 +229,49 @@
             device_id={"patch": near}, device_id_type=MESH,
         )
 
-    def z_copy(i, zt, src):
-        return pltpu.make_async_remote_copy(
-            src_ref=zsend.at[i], dst_ref=zrecv.at[src], send_sem=z_s.at[i], recv_sem=z_r.at[src],
-            device_id={"patch": zt * 2 + x}, device_id_type=MESH,
-        )
+    order = (3 * (1 - z // 2), (2 + 3 * z) % 5, 1 + z % 2, z)
+
+    def z_copy(dest):
+        up = dest > z
+        after = jnp.where(up, z + 1, z - 1)
+        slot = jnp.where(jnp.logical_and(dest < z, after == dest), zs, dest)
+        return pltpu.make_async_remote_copy(
+            src_ref=zsend.at[dest], dst_ref=zrecv.at[slot], send_sem=z_s.at[dest], recv_sem=z_r.at[slot],
+            device_id={"patch": after * 2 + x}, device_id_type=MESH,
+        )
+
+    def z_arrival(slot):
+        return pltpu.make_async_copy(zrecv.at[slot], zrecv.at[slot], z_r.at[slot])
 
     def forward(i):
+        dest = order[i]
         x_copy(i).wait_recv()
-        zsend[i] = (keep[i] + xrecv[i].astype(F32)).astype(BF)
-        z_copy(i, (z + 1 + i) % zs, z).start()
-
-    @pl.loop(0, zs)
-    def _(i):
-        def put(cols, s):
+        upward = jnp.logical_and(dest > z, z > 0)
+        downward = jnp.logical_and(dest < z, z < zs - 1)
+
+        @pl.when(jnp.logical_or(upward, downward))
+        def _():
+            z_arrival(dest).wait()
+            keep[i] += zrecv[dest].astype(F32)
+
+        zsend[dest] = (keep[i] + xrecv[i].astype(F32)).astype(BF)
+        z_copy(dest).start()
+
+    for i in range(zs):
+        def put(cols, s, i=i):
             xsend[i, :, cols] = s.astype(BF)
 
-        conv((z + 1 + i) % zs * 2 + 1 - x, put)
+        conv(order[i] * 2 + 1 - x, put)
         x_copy(i).start()
 
-    @pl.loop(0, zs)
-    def _(i):
-        def put(cols, s):
+    for i in range(zs):
+        def put(cols, s, i=i):
             keep[i, :, cols] = s
 
-        conv((z + 1 + i) % zs * 2 + x, put)
-
-    forward(0)
+        conv(order[i] * 2 + x, put)
+
+    for i in range(zs - 1):
+        forward(i)
 
     @pl.loop(0, 9)
     def _(t):
@@ -277,8 +293,6 @@
         src = (z + k) % zs * 2 + x
         u_copy(src, src).wait_recv()
         u_pass(src).start()
-    for i in range(1, zs - 1):
-        forward(i)
     dp_copy(mate).wait_recv()
     for q in range(reqs // 2):
         pair = []
@@ -319,10 +333,17 @@
     up_copy(core).start()
     x_copy(zs - 1).wait_recv()
     out[...] = skip[...] + keep[zs - 1] + xrecv[zs - 1].astype(F32)
-    for k in range(1, zs):
-        src = (z + k) % zs
-        z_copy(0, src, src).wait_recv()
-        out[...] += zrecv[src].astype(F32)
+
+    @pl.when(z > 0)
+    def _():
+        z_arrival(z).wait()
+        out[...] += zrecv[z].astype(F32)
+
+    @pl.when(z < zs - 1)
+    def _():
+        z_arrival(zs).wait()
+        out[...] += zrecv[zs].astype(F32)
+
     up_copy(mate).wait_recv()
     both = lsend[me].astype(F32)
     for k in range(1, n):
@@ -357,9 +378,8 @@
     def _(i):
         x_copy(i).wait_send()
 
-    @pl.loop(0, zs - 1)
-    def _(i):
-        z_copy(i, (z + 1 + i) % zs, z).wait_send()
+    for i in range(zs - 1):
+        z_copy(order[i]).wait_send()
 
 
 def run_block(n, steps, asked, row_of, hid, skip, table, gain, bias, weight, down, up):
@@ -390,8 +410,8 @@
             pltpu.VMEM((zs, cells, chans), BF),
             pltpu.VMEM((zs, cells, chans), BF),
             pltpu.VMEM((zs, cells, chans), F32),
-            pltpu.VMEM((zs - 1, cells, chans), BF),
             pltpu.VMEM((zs, cells, chans), BF),
+            pltpu.VMEM((zs + 1, cells, chans), BF),
             pltpu.VMEM((n, cells // 2, 2 * rank), BF),
             pltpu.VMEM((n, cells // 2, 2 * rank), BF),
             dma((n,)), dma((n,)),
@@ -400,7 +420,7 @@
             dma((9,)), dma((9,)), dma((9,)),
             dma, dma,
             dma((zs,)), dma((zs,)),
-            dma((zs - 1,)), dma((zs,)),
+            dma((zs,)), dma((zs + 1,)),
             dma((n,)), dma((n,)),
             dma((n,)), dma((n,)), dma((n,)), dma,
             dma, dma,
@@ -432,7 +452,7 @@
     own = kernel_weight.shape[1]
     ends = all(j * own // LANES * LANES + WIN <= hidden.shape[3] and j * own % LANES + own <= WIN for j in range(n))
     return (
-        n % 2 == 0 and n <= 8 and hidden.shape[1] == 1 and hidden.shape[0] in (2, 4, 6, 8)
+        n == 8 and hidden.shape[1] == 1 and hidden.shape[0] in (2, 4, 6, 8)
         and own % 32 == 0 and ends and down.shape[1] == 64
     )
 

time: 182 us -> 151 us (0.83)
  Pallas kernels: 177 us -> 145 us
    pallas_call x1, Pallas kernels: 177 us -> 145 us  [run_block(): pl.pallas_call(functools.partial(block_kernel, n, own, reqs, width, chans...]
where the time goes in v3:
time: 151 us; the launch traced here: 150 us
  Pallas kernels  145 us (96%)
  local copies, waits for them, and re-layouts  5.08 us (3%)
    pallas_call x1, Pallas kernels, run_block(): pl.pallas_call(functools.partial(block_kernel, n, own, reqs, width, chans...  145 us

profile of v3, /device:TPU:25, one launch (start us, length us, event | category | flops | bytes accessed | tf_op | source)
XLA Modules:
  0.0 150.5 jit_solution(17603944300842358985)
XLA Ops:
  0.0 1.3 broadcast_in_dim.6.gain
  1.3 1.3 broadcast_in_dim.7.bias
  2.6 145.4 %shard_map.109 = f32[256,1280]{1,0:T(8,128)} custom-call(s32[4]{0:T(128)} %steps.1, s32[4]{0:T(128)} %asked.1, s32[16]{0:T(128)} %row_of.1, f32[256,1280]{1,0:T(8,128)} %bitcast.6, f32[256,1280]{1,0:T(8,128)} %bitcast.7, f32[50,1280]{1,0:T(8,128)} %table.1, f32[1,1280]{1,0:T(1,128)} %broadcast_in_dim.6.gain, f32[1,1280]{1,0:T(1,128)} %broadcast_in_dim.7.bias, ...), custom_call_target="tpu_custom_call" | custom-call | flops 12079595520 | bytes 100000000 | tf_op jit(solution)/shard_map/pallas_call | solution.py:396
  148.0 2.5 %copy.14 = f32[4,1,64,1280]{3,2,1,0:T(8,128)} copy(f32[4,1,64,1280]{3,2,1,0:T(8,128)} %bitcast.5) | data formatting | bytes 2621440

commit v4 on v3

--- a/solution.py
+++ b/solution.py
@@ -25,7 +25,7 @@
     n, own, reqs, width, chans,
     steps, asked, row_of, hid, skip, table, gain, bias, w_hbm, d_hbm, u_hbm,
     out,
-    act, acts_in, taps, wpad, dall, uall, stat_out, stat_in,
+    act, acts_in, taps, wpad, dfull, dpack, dall, uall, stat_out, stat_in,
     xsend, xrecv, keep, zsend, zrecv, lsend, lrecv,
     st_s, st_r, ac_s, ac_r, ac_l, d_s, d_r, d_l, w_s, w_r, w_l, dp_s, dp_r,
     x_s, x_r, z_s, z_r, l_s, l_r, u_s, u_f, u_r, u_l, up_s, up_r,
@@ -77,30 +77,26 @@
 
     rank_at = pl.multiple_of(core * hrank, hrank)
 
-    def d_src(t, peer):
-        return d_hbm.at[:, pl.ds(rank_at, hrank), pl.ds(pl.multiple_of(t * chans + window(peer), LANES), WIN)]
-
-    def d_dst(t, src):
-        return dall.at[pl.ds(src * per, per), pl.ds(rank_at, hrank), pl.ds(pl.multiple_of(t * WIN, WIN), WIN)]
-
-    def d_copy(t, peer, src):
-        return pltpu.make_async_remote_copy(
-            src_ref=d_src(t, peer), dst_ref=d_dst(t, src),
-            send_sem=d_s.at[peer, t], recv_sem=d_r.at[src, t],
+    def d_dst(src):
+        return dall.at[pl.ds(src * per, per), pl.ds(rank_at, hrank), :]
+
+    def d_copy(peer, src):
+        return pltpu.make_async_remote_copy(
+            src_ref=dpack.at[peer], dst_ref=d_dst(src),
+            send_sem=d_s.at[peer], recv_sem=d_r.at[src],
             device_id={"patch": peer}, device_id_type=MESH,
         )
 
-    def d_own(t):
-        return pltpu.make_async_copy(d_src(t, me), d_dst(t, me), d_l.at[t])
-
-    def send_down(lo, hi):
-        @pl.loop(lo, hi)
-        def _(t):
-            d_own(t).start()
-
-            @pl.loop(1, n)
-            def _(k):
-                d_copy(t, (me + k) % n, me).start()
+    d_load = pltpu.make_async_copy(d_hbm.at[:, pl.ds(rank_at, hrank), :], dfull, d_l)
+    d_load.start()
+    d_load.wait()
+    for a in range(per):
+        for j in range(n):
+            parts = [dfull[a, :, t * chans + j * own : t * chans + (j + 1) * own] for t in range(9)]
+            dpack[j, a] = jnp.concatenate(parts, axis=1)
+    for k in range(1, n):
+        d_copy((me + k) % n, me).start()
+    d_dst(me)[...] = dpack[me]
 
     def u_dst(src):
         return uall.at[pl.ds(src * per, per), pl.ds(rank_at, hrank), :]
@@ -127,8 +123,6 @@
         u_copy(near, me).start()
         for k in range(1, zs):
             u_copy((z + k) % zs * 2 + x, me).start()
-
-    send_down(0, 3)
 
     c_of = lax.broadcasted_iota(jnp.int32, (chans, LANES), 0)
     g_of = lax.broadcasted_iota(jnp.int32, (chans, LANES), 1)
@@ -185,7 +179,6 @@
         ac_copy((me + k) % n, me).start()
     ac_own.start()
 
-    send_down(3, 9)
     send_up()
 
     taps[0] = jnp.zeros(taps.shape[1:], BF)
@@ -273,13 +266,8 @@
     for i in range(zs - 1):
         forward(i)
 
-    @pl.loop(0, 9)
-    def _(t):
-        d_own(t).wait()
-
-        @pl.loop(1, n)
-        def _(k):
-            d_copy(t, (me + k) % n, (me + k) % n).wait_recv()
+    for k in range(1, n):
+        d_copy((me + k) % n, (me + k) % n).wait_recv()
 
     def dp_copy(at):
         part = dall.at[:, pl.ds(pl.multiple_of(at * hrank, hrank), hrank), :]
@@ -297,7 +285,13 @@
     for q in range(reqs // 2):
         pair = []
         for r in (2 * q, 2 * q + 1):
-            factor = dall[sel[r]]
+            packed = dall[sel[r]].astype(F32)
+            empty = jnp.zeros((rank, WIN - own), F32)
+            spread_out = [
+                pltpu.roll(jnp.concatenate([packed[:, t * own : (t + 1) * own], empty], axis=1), inner, 1)
+                for t in range(9)
+            ]
+            factor = jnp.concatenate(spread_out, axis=1).astype(BF)
             low = jnp.zeros((n * width, rank), F32)
             for dy in range(3):
                 lhs = taps[dy : dy + n, r * width : (r + 1) * width, :].reshape(n * width, 3 * WIN)
@@ -368,11 +362,8 @@
         ac_copy((me + k) % n, me).wait_send()
         l_copy((me + k) % n, me).wait_send()
 
-    @pl.loop(0, 9)
-    def _(t):
-        @pl.loop(1, n)
-        def _(k):
-            d_copy(t, (me + k) % n, me).wait_send()
+    for k in range(1, n):
+        d_copy((me + k) % n, me).wait_send()
 
     @pl.loop(0, zs)
     def _(i):
@@ -403,7 +394,9 @@
             pltpu.VMEM((n, cells, WIN), BF),
             pltpu.VMEM((n + 2, cells, 3 * WIN), BF),
             pltpu.VMEM((3, 3 * WIN, chans), BF),
-            pltpu.VMEM((n * per, rank, 9 * WIN), BF),
+            pltpu.VMEM((per, rank // 2, 9 * chans), BF),
+            pltpu.VMEM((n, per, rank // 2, 9 * own), BF),
+            pltpu.VMEM((n * per, rank, 9 * own), BF),
             pltpu.VMEM((n * per, rank, chans), BF),
             pltpu.VMEM((2, 8, LANES), F32),
             pltpu.VMEM((n, 2, 8, LANES), F32),
@@ -416,7 +409,7 @@
             pltpu.VMEM((n, cells // 2, 2 * rank), BF),
             dma((n,)), dma((n,)),
             dma((n,)), dma((n,)), dma,
-            dma((n, 9)), dma((n, 9)), dma((9,)),
+            dma((n,)), dma((n,)), dma,
             dma((9,)), dma((9,)), dma((9,)),
             dma, dma,
             dma((zs,)), dma((zs,)),

time: 151 us -> 161 us (1.066)
  Pallas kernels: 145 us -> 156 us
    pallas_call x1, Pallas kernels: 145 us -> 156 us  [run_block(): pl.pallas_call(functools.partial(block_kernel, n, own, reqs, width, chans...]
where the time goes in v4:
time: 161 us
  Pallas kernels  156 us (97%)
  local copies, waits for them, and re-layouts  5.08 us (3%)
    pallas_call x1, Pallas kernels, run_block(): pl.pallas_call(functools.partial(block_kernel, n, own, reqs, width, chans...  156 us

profile of v4, /device:TPU:25, one launch (start us, length us, event | category | flops | bytes accessed | tf_op | source)
XLA Modules:
  0.0 161.1 jit_solution(10811045478294878184)
XLA Ops:
  0.0 1.3 broadcast_in_dim.6.gain
  1.3 1.3 broadcast_in_dim.7.bias
  2.6 156.0 %shard_map.109 = f32[256,1280]{1,0:T(8,128)} custom-call(s32[4]{0:T(128)} %steps.1, s32[4]{0:T(128)} %asked.1, s32[16]{0:T(128)} %row_of.1, f32[256,1280]{1,0:T(8,128)} %bitcast.6, f32[256,1280]{1,0:T(8,128)} %bitcast.7, f32[50,1280]{1,0:T(8,128)} %table.1, f32[1,1280]{1,0:T(1,128)} %broadcast_in_dim.6.gain, f32[1,1280]{1,0:T(1,128)} %broadcast_in_dim.7.bias, ...), custom_call_target="tpu_custom_call" | custom-call | flops 12079595520 | bytes 100000000 | tf_op jit(solution)/shard_map/pallas_call | solution.py:387
  158.6 2.5 %copy.14 = f32[4,1,64,1280]{3,2,1,0:T(8,128)} copy(f32[4,1,64,1280]{3,2,1,0:T(8,128)} %bitcast.5) | data formatting | bytes 2621440
